TPU v7x, 128 devices: a whole 4x4x4 slice. The times are simulated.
128 devices in a mesh: curve: 128 (over y, x, z, core).
Axes of the slice: x: 4, y: 4, z: 4, core: 2. Of those that a mesh axis runs over, the one named last changes fastest.
Arguments:
- diag_blocks: bfloat16 [8192, 128, 128], P('curve'), may hold values from 0.049804688 to 1
- super_blocks: bfloat16 [8192, 4, 128, 128], P('curve'), may hold values from 0.049804688 to 1
- far_blocks: bfloat16 [32768, 128, 128], P('curve'), may hold values from 0.049804688 to 1
- far_row: int32 [32768], P('curve'), may hold values from -1 to 63, as said below
- send_slot: int32 [32768], P('curve'), may hold values from -1 to 63, as said below
- start_panel: float32 [64, 1048576], P(None, 'curve'), may hold values from -6 to 6
Outputs:
- basis: float32 [64, 1048576], P(None, 'curve')
- update: float32 [64, 1048576], P(None, 'curve')
Inputs may be any that keep to these rules, and one draw needn't show every extreme that they name: `send_slot`: at most 2 live slots from one owner to one reader; some owner fills all 2 slots to every reader. `far_row`: empty slots match those of send_slot.
All inputs are finite; a program needn't handle non-finite values.
Results may differ from a plain program's by a relative error of at most 0.0026.
Values may be sent and summed in bfloat16 or wider, within the bound.
A program may use at most 256 MiB of HBM per device.

v0:
```python
import jax
import jax.numpy as jnp
from jax import lax
from jax.sharding import PartitionSpec as P

ITERS = 2
exact_mode = lax.Precision.HIGHEST
step_size = 10.0
momentum = 0.5


def extended_2(array, sides, width):
    for axis, dim in sides:
        size, length = (lax.axis_size(axis), array.shape[dim])
        up = [(i, (i + 1) % size) for i in range(size)]
        down = [(j, i) for i, j in up]
        last = lax.slice_in_dim(array, length - width, length, axis=dim)
        initial = lax.slice_in_dim(array, 0, width, axis=dim)
        before = lax.ppermute(last, axis, up)
        after = lax.ppermute(initial, axis, down)
        array = jnp.concatenate([before, array, after], axis=dim)
    return array


def passed_along(block, axis, distance):
    devices = range(lax.axis_size(axis))
    route = [((i - distance) % len(devices), i) for i in devices]
    return lax.ppermute(block, axis, route)


def gram_of(first, second):
    return jnp.einsum("bip,bjp->ij", first, second, precision=exact_mode)


def lower_inverse(cross):
    factor = jnp.linalg.cholesky(cross)
    return lax.linalg.triangular_solve(
        factor, jnp.eye(cross.shape[0], dtype=cross.dtype), left_side=True, lower=True
    )


def left_apply(matrix, blocks):
    return jnp.einsum("ij,bjp->bip", matrix, blocks, precision=exact_mode)


def near_apply(panel, diag_blocks, super_blocks, edge_supers):
    bands = super_blocks.shape[1]
    rows_dev = panel.shape[0]
    extended = extended_2(panel, (("curve", 0),), bands)
    supers_ext = jnp.concatenate([edge_supers, super_blocks], axis=0)
    result = jnp.einsum("bcp,bqp->bcq", panel, diag_blocks, preferred_element_type=jnp.float32)
    result = result + jnp.einsum(
        "bcp,bpq->bcq", panel, diag_blocks, preferred_element_type=jnp.float32
    )
    for band in range(bands):
        ahead = extended[bands + band + 1 : bands + band + 1 + rows_dev]
        result = result + jnp.einsum(
            "bcp,bqp->bcq", ahead, super_blocks[:, band], preferred_element_type=jnp.float32
        )
        first = bands - band - 1
        behind = extended[first : first + rows_dev]
        result = result + jnp.einsum(
            "bcp,bpq->bcq",
            behind,
            supers_ext[first : first + rows_dev, band],
            preferred_element_type=jnp.float32,
        )
    return result


def shards(diag_blocks, super_blocks, far_blocks, far_row, send_slot, start_panel):
    bands = super_blocks.shape[1]
    rows_dev = diag_blocks.shape[0]
    block_size = diag_blocks.shape[1]
    width = start_panel.shape[0]
    total_points = rows_dev * block_size * lax.axis_size("curve")
    edge_supers = passed_along(super_blocks[rows_dev - bands :], "curve", 1)
    send_live = (send_slot >= 0)[:, None, None]
    send_index = jnp.maximum(send_slot, 0)
    recv_live = (far_row >= 0)[:, None, None]
    recv_index = jnp.maximum(far_row, 0)

    def apply_w(panel):
        result = near_apply(panel, diag_blocks, super_blocks, edge_supers)
        outgoing = jnp.where(send_live, panel[send_index], jnp.zeros((), jnp.bfloat16))
        incoming = lax.all_to_all(outgoing, "curve", split_axis=0, concat_axis=0, tiled=True)
        forward = jnp.einsum(
            "fcp,fqp->fcq", incoming, far_blocks, preferred_element_type=jnp.float32
        )
        result = result.at[recv_index].add(jnp.where(recv_live, forward, 0.0))
        mirror = jnp.einsum(
            "fcp,fpq->fcq", panel[recv_index], far_blocks, preferred_element_type=jnp.float32
        )
        mirror = jnp.where(recv_live, mirror, 0.0)
        returned = lax.all_to_all(mirror, "curve", split_axis=0, concat_axis=0, tiled=True)
        result = result.at[send_index].add(jnp.where(send_live, returned, 0.0))
        return result

    unit_panel = jnp.ones((rows_dev, 1, block_size), jnp.bfloat16)
    inv_root = lax.rsqrt(apply_w(unit_panel))
    start_blocks = start_panel.reshape(width, rows_dev, block_size).transpose(1, 0, 2)
    start_gram = lax.psum(gram_of(start_blocks, start_blocks), "curve") / total_points
    current = left_apply(lower_inverse(start_gram), start_blocks)
    change = jnp.zeros_like(current)
    for step in range(ITERS):
        scaled = (inv_root * current).astype(jnp.bfloat16)
        image = inv_root * apply_w(scaled)
        rayleigh = lax.psum(gram_of(current, image), "curve") / total_points
        resid = image - left_apply(rayleigh.T, current)
        trial = current + step_size * resid + momentum * change
        cross = lax.psum(gram_of(trial, trial), "curve") / total_points
        fresh = left_apply(lower_inverse(cross), trial)
        change = fresh - current
        current = fresh
    basis = current.transpose(1, 0, 2).reshape(width, rows_dev * block_size)
    update = change.transpose(1, 0, 2).reshape(width, rows_dev * block_size)
    return (basis, update)


def solution(mesh):
    return jax.shard_map(
        shards,
        mesh=mesh,
        in_specs=(
            P("curve", None, None),
            P("curve", None, None, None),
            P("curve", None, None),
            P("curve"),
            P("curve"),
            P(None, "curve"),
        ),
        out_specs=(P(None, "curve"), P(None, "curve")),
        check_vma=False,
    )
```

profile of v0, /device:TPU:1, one launch (start us, length us, event | category | flops | bytes accessed | tf_op | source)
XLA Modules:
  0.0 952.7 jit_solution(4395993751826965920)
XLA Ops:
  7.6 10.2 %all-to-all-start = ((bf16[128,2,128]{2,1,0:T(2,128)(2,1)}), bf16[128,2,128]{2,1,0:T(2,128)(2,1)S(1)}, u32[]{:S(2)}, u32[]{:S(2)}) async-start(bf16[128,2,128]{2,1,0:T(2,128)(2,1)} %bitcast.265), calls=%async_computation | async-start | bytes 131072 | tf_op jit(solution)/shard_map/all_to_all | solution.py:86
  17.8 10.4 %copy.58 = bf16[64,4,128,128]{3,2,0,1:T(8,128)(2,1)} copy(bf16[64,4,128,128]{3,2,1,0:T(8,128)(2,1)} %param.10) | data formatting | bytes 16777216 | tf_op args[1]
  36.0 66.3 %psum.35 = f32[64,64]{0,1:T(8,128)S(1)} all-reduce(f32[64,64]{0,1:T(8,128)S(1)} %fusion.51), channel_id=1, replica_groups=mesh['curve'=128] {'curve'}, use_global_device_ids=true, to_apply=%region_0.1 | all-reduce | flops 4096 | bytes 32768 | tf_op jit(solution)/shard_map/psum | solution.py:102
  102.4 5.8 cholesky.59
  137.4 6.0 all-to-all-start.1
  144.3 7.8 fusion.66
  153.0 10.5 %constant_dynamic-update-slice_fusion = bf16[68,4,128,128]{3,2,0,1:T(8,128)(2,1)} fusion(bf16[68,4,128,128]{3,2,0,1:T(8,128)(2,1)} %constant_dynamic-update-slice_fusion.1, bf16[64,4,128,128]{3,2,1,0:T(8,128)(2,1)} %param.10), kind=kLoop, calls=%fused_computation.180 | loop fusion | bytes 16777216 | tf_op jit(solution)/shard_map/concatenate | solution.py:50
  196.9 11.0 %all-to-all-start.2 = ((bf16[256,64,128]{2,1,0:T(8,128)(2,1)}), bf16[256,64,128]{2,1,0:T(8,128)(2,1)}, u32[]{:S(2)}, u32[]{:S(2)}) async-start(bf16[256,64,128]{2,1,0:T(8,128)(2,1)} %broadcast_select_fusion.7), calls=%async_computation.2 | async-start | bytes 8388608 | tf_op jit(solution)/shard_map/all_to_all | solution.py:86
  207.9 10.3 %broadcast_select_fusion.4 = f32[256,64,128]{2,1,0:T(8,128)} fusion(pred[256]{0:T(512)(128)(4,1)S(1)} %broadcast_compare_fusion.1, bf16[256,64,128]{2,1,0:T(8,128)(2,1)} %gather_fusion.3, bf16[256,128,128]{2,1,0:T(8,128)(2,1)} %param.11), kind=kOutput, calls=%fused_computation.16 | convolution fusion | flops 538968064 | bytes 20971776 | tf_op jit(solution)/shard_map/fcp,fpq->fcq/dot_general | solution.py:91
  233.9 26.7 %all-to-all-done.2 = bf16[256,64,128]{2,1,0:T(8,128)(2,1)} async-done(((bf16[256,64,128]{2,1,0:T(8,128)(2,1)}), bf16[256,64,128]{2,1,0:T(8,128)(2,1)}, u32[]{:S(2)}, u32[]{:S(2)}) %all-to-all-start.2) | async-done | bytes 4194336 | tf_op jit(solution)/shard_map/all_to_all | solution.py:86
  260.6 6.3 all-to-all-start.3
  280.3 6.1 add_add_fusion.1
  286.5 11.3 %broadcast_select_fusion.5 = f32[256,64,128]{2,1,0:T(8,128)} fusion(pred[256]{0:T(512)(128)(4,1)S(1)} %copy-done.18, bf16[256,64,128]{2,1,0:T(8,128)(2,1)} %all-to-all-done.2, bf16[256,128,128]{2,1,0:T(8,128)(2,1)S(1)} %bitcast.267), kind=kOutput, calls=%fused_computation.17 | convolution fusion | flops 538968064 | bytes 20971776 | tf_op jit(solution)/shard_map/fcp,fqp->fcq/dot_general | solution.py:87
  297.8 38.8 %scatter_fusion = f32[64,64,128]{2,1,0:T(8,128)} fusion(f32[64,64,128]{2,1,0:T(8,128)} %add_add_fusion.1, s32[256]{0:T(256)S(1)} %copy-done.31, f32[256,64,128]{2,1,0:T(8,128)} %broadcast_select_fusion.5), kind=kCustom, calls=%fused_computation.8 | custom fusion | flops 2097152 | bytes 25166848 | tf_op jit(solution)/shard_map/scatter-add | solution.py:90
  336.6 31.6 %all-to-all-done.3 = f32[256,64,128]{2,1,0:T(8,128)} async-done(((f32[256,64,128]{2,1,0:T(8,128)}), f32[256,64,128]{2,1,0:T(8,128)}, u32[]{:S(2)}, u32[]{:S(2)}) %all-to-all-start.3) | async-done | bytes 8388640 | tf_op jit(solution)/shard_map/all_to_all | solution.py:95
  368.2 6.0 broadcast_select_fusion.3
  374.3 39.0 %scatter_fusion.1 = f32[64,64,128]{2,1,0:T(8,128)} fusion(f32[64,64,128]{2,1,0:T(8,128)} %scatter_fusion, s32[256]{0:T(256)S(1)} %copy-done.28, f32[256,64,128]{2,1,0:T(8,128)} %broadcast_select_fusion.3), kind=kCustom, calls=%fused_computation.9 | custom fusion | flops 2097152 | bytes 25166848 | tf_op jit(solution)/shard_map/scatter-add | solution.py:96
  417.4 66.9 %psum.36 = f32[64,64]{0,1:T(8,128)S(1)} all-reduce(f32[64,64]{0,1:T(8,128)S(1)} %fusion.52), channel_id=1, replica_groups=mesh['curve'=128] {'curve'}, use_global_device_ids=true, to_apply=%region_7.10 | all-reduce | flops 4096 | bytes 32768 | tf_op jit(solution)/shard_map/psum | solution.py:108
  492.5 63.1 %psum.37 = f32[64,64]{0,1:T(8,128)S(1)} all-reduce(f32[64,64]{0,1:T(8,128)S(1)} %convolution_bitcast_fusion.3), channel_id=1, replica_groups=mesh['curve'=128] {'curve'}, use_global_device_ids=true, to_apply=%region_8.11 | all-reduce | flops 4096 | bytes 32768 | tf_op jit(solution)/shard_map/psum | solution.py:111
  555.7 5.8 cholesky.70
  587.5 11.4 %all-to-all-start.4 = ((bf16[256,64,128]{2,1,0:T(8,128)(2,1)}), bf16[256,64,128]{2,1,0:T(8,128)(2,1)}, u32[]{:S(2)}, u32[]{:S(2)}) async-start(bf16[256,64,128]{2,1,0:T(8,128)(2,1)} %broadcast_select_fusion.6), calls=%async_computation.4 | async-start | bytes 8388608 | tf_op jit(solution)/shard_map/all_to_all | solution.py:86
  598.8 10.3 %broadcast_select_fusion.1 = f32[256,64,128]{2,1,0:T(8,128)} fusion(pred[256]{0:T(512)(128)(4,1)S(1)} %copy-done.18, bf16[256,64,128]{2,1,0:T(8,128)(2,1)} %gather_fusion.5, bf16[256,128,128]{2,1,0:T(8,128)(2,1)} %param.11), kind=kOutput, calls=%fused_computation.13 | convolution fusion | flops 538968064 | bytes 20971776 | tf_op jit(solution)/shard_map/fcp,fpq->fcq/dot_general | solution.py:91
  624.8 26.8 %all-to-all-done.4 = bf16[256,64,128]{2,1,0:T(8,128)(2,1)} async-done(((bf16[256,64,128]{2,1,0:T(8,128)(2,1)}), bf16[256,64,128]{2,1,0:T(8,128)(2,1)}, u32[]{:S(2)}, u32[]{:S(2)}) %all-to-all-start.4) | async-done | bytes 4194336 | tf_op jit(solution)/shard_map/all_to_all | solution.py:86
  651.6 6.3 all-to-all-start.5
  676.2 11.3 %broadcast_select_fusion.2 = f32[256,64,128]{2,1,0:T(8,128)} fusion(pred[256]{0:T(512)(128)(4,1)S(1)} %copy-done.19, bf16[256,64,128]{2,1,0:T(8,128)(2,1)} %all-to-all-done.4, bf16[256,128,128]{2,1,0:T(8,128)(2,1)S(1)} %bitcast.269), kind=kOutput, calls=%fused_computation.14 | convolution fusion | flops 538968064 | bytes 20971776 | tf_op jit(solution)/shard_map/fcp,fqp->fcq/dot_general | solution.py:87
  687.5 26.2 %scatter_fusion.2 = f32[64,64,128]{2,1,0:T(8,128)S(1)} fusion(f32[64,64,128]{2,1,0:T(8,128)S(1)} %add_add_fusion, s32[256]{0:T(256)S(1)} %copy-done.32, f32[256,64,128]{2,1,0:T(8,128)} %broadcast_select_fusion.2), kind=kCustom, calls=%fused_computation.10 | custom fusion | flops 2097152 | bytes 25166848 | tf_op jit(solution)/shard_map/scatter-add | solution.py:90
  713.7 45.4 %all-to-all-done.5 = f32[256,64,128]{2,1,0:T(8,128)} async-done(((f32[256,64,128]{2,1,0:T(8,128)}), f32[256,64,128]{2,1,0:T(8,128)}, u32[]{:S(2)}, u32[]{:S(2)}) %all-to-all-start.5) | async-done | bytes 8388640 | tf_op jit(solution)/shard_map/all_to_all | solution.py:95
  759.2 6.0 broadcast_select_fusion
  765.2 26.1 %scatter_fusion.3 = f32[64,64,128]{2,1,0:T(8,128)S(1)} fusion(f32[64,64,128]{2,1,0:T(8,128)S(1)} %scatter_fusion.2, s32[256]{0:T(256)S(1)} %copy-done.29, f32[256,64,128]{2,1,0:T(8,128)} %broadcast_select_fusion), kind=kCustom, calls=%fused_computation.11 | custom fusion | flops 2097152 | bytes 25166848 | tf_op jit(solution)/shard_map/scatter-add | solution.py:96
  794.9 66.9 %psum.38 = f32[64,64]{0,1:T(8,128)S(1)} all-reduce(f32[64,64]{0,1:T(8,128)S(1)} %fusion.57), channel_id=1, replica_groups=mesh['curve'=128] {'curve'}, use_global_device_ids=true, to_apply=%region_11.14 | all-reduce | flops 4096 | bytes 32768 | tf_op jit(solution)/shard_map/psum | solution.py:108
  870.3 63.1 %psum.39 = f32[64,64]{0,1:T(8,128)S(1)} all-reduce(f32[64,64]{0,1:T(8,128)S(1)} %convolution_bitcast_fusion.1), channel_id=1, replica_groups=mesh['curve'=128] {'curve'}, use_global_device_ids=true, to_apply=%region_12.15 | all-reduce | flops 4096 | bytes 32768 | tf_op jit(solution)/shard_map/psum | solution.py:111
  933.5 5.8 cholesky.81
  (228 shorter events, 205.5 us)
Async XLA Ops:
  0.6 30.5 %copy-start = (bf16[64,128,128]{2,1,0:T(8,128)(2,1)S(1)}, bf16[64,128,128]{2,1,0:T(8,128)(2,1)}, u32[]{:S(2)}) copy-start(bf16[64,128,128]{2,1,0:T(8,128)(2,1)} %param.9) | copy-start | bytes 6291460
  0.7 135.5 %collective-permute-start.1 = (bf16[4,1,128]{2,0,1:T(4,128)(2,1)S(1)}, bf16[4,1,128]{2,0,1:T(4,128)(2,1)S(1)}, u32[]{:S(2)}, u32[]{:S(2)}) collective-permute-start(bf16[4,1,128]{2,0,1:T(4,128)(2,1)S(1)} %broadcast.92), channel_id=1, source_target_pairs={{0,1},{1,2},{2,3},{3,4},{4,5},{5,6},{6,7},{7,8},{8,9},{9,10},{10,1... | collective-permute-start | bytes 3080 | tf_op jit(solution)/shard_map/ppermute | solution.py:19
  3.8 118.8 %collective-permute-start = (bf16[4,1,128]{2,0,1:T(4,128)(2,1)S(1)}, bf16[4,1,128]{2,0,1:T(4,128)(2,1)S(1)}, u32[]{:S(2)}, u32[]{:S(2)}) collective-permute-start(bf16[4,1,128]{2,0,1:T(4,128)(2,1)S(1)} %broadcast.92), channel_id=1, source_target_pairs={{1,0},{2,1},{3,2},{4,3},{5,4},{6,5},{7,6},{8,7},{9,8},{10,9},{11,1... | collective-permute-start | bytes 3080 | tf_op jit(solution)/shard_map/ppermute | solution.py:20
  4.4 188.4 %copy-start.24 = (pred[256]{0:T(512)(128)(4,1)}, pred[256]{0:T(512)(128)(4,1)S(1)}, u32[]{:S(2)}) copy-start(pred[256]{0:T(512)(128)(4,1)S(1)} %broadcast_compare_fusion) | copy-start | bytes 772
  5.1 169.7 %copy-start.27 = (s32[256]{0:T(256)}, s32[256]{0:T(256)S(1)}, u32[]{:S(2)}) copy-start(s32[256]{0:T(256)S(1)} %broadcast_maximum_fusion) | copy-start | bytes 3076
  5.8 166.9 %copy-start.30 = (s32[256]{0:T(256)}, s32[256]{0:T(256)S(1)}, u32[]{:S(2)}) copy-start(s32[256]{0:T(256)S(1)} %broadcast_maximum_fusion.1) | copy-start | bytes 3076
  5.8 108.6 %copy-start.38 = (s32[1024]{0:T(1024)}, s32[1024]{0:T(1024)S(1)}, u32[]{:S(2)}) copy-start(s32[1024]{0:T(1024)S(1)} %get-tuple-element.20) | copy-start | bytes 12292
  7.6 129.2 %all-to-all-start = ((bf16[128,2,128]{2,1,0:T(2,128)(2,1)}), bf16[128,2,128]{2,1,0:T(2,128)(2,1)S(1)}, u32[]{:S(2)}, u32[]{:S(2)}) async-start(bf16[128,2,128]{2,1,0:T(2,128)(2,1)} %bitcast.265), calls=%async_computation | async-start | bytes 131072 | tf_op jit(solution)/shard_map/all_to_all | solution.py:86
  17.8 13.3 %copy-start.39 = (s32[256]{0:T(256)S(1)}, s32[256]{0:T(256)}, u32[]{:S(2)}) copy-start(s32[256]{0:T(256)} %param.12) | copy-start | bytes 3076
  29.3 122.8 %collective-permute-start.2 = (bf16[4,4,128,128]{3,2,0,1:T(8,128)(2,1)S(1)}, bf16[4,4,128,128]{3,2,0,1:T(8,128)(2,1)S(1)}, u32[]{:S(2)}, u32[]{:S(2)}) collective-permute-start(bf16[4,4,128,128]{3,2,0,1:T(8,128)(2,1)S(1)} %slice.207), channel_id=1, source_target_pairs={{127,0},{0,1},{1,2},{2,3},{3,4},{4,5},{5,6},{6,7},{7,8},{8,9},{9,1... | collective-permute-start | bytes 1572872 | tf_op jit(solution)/shard_map/ppermute | solution.py:28
  31.1 176.7 %copy-start.17 = (pred[256]{0:T(512)(128)(4,1)}, pred[256]{0:T(512)(128)(4,1)S(1)}, u32[]{:S(2)}) copy-start(pred[256]{0:T(512)(128)(4,1)S(1)} %broadcast_compare_fusion.1) | copy-start | bytes 772
  137.4 37.4 %all-to-all-start.1 = ((f32[256,1,128]{2,1,0:T(1,128)}), f32[256,1,128]{2,1,0:T(1,128)S(1)}, u32[]{:S(2)}, u32[]{:S(2)}) async-start(f32[256,1,128]{2,1,0:T(1,128)} %bitcast.58), calls=%async_computation.1 | async-start | bytes 262144 | tf_op jit(solution)/shard_map/all_to_all | solution.py:95
  190.9 76.0 %collective-permute-start.4 = (bf16[4,64,128]{2,1,0:T(8,128)(2,1)}, bf16[4,64,128]{2,1,0:T(8,128)(2,1)}, u32[]{:S(2)}, u32[]{:S(2)}) collective-permute-start(bf16[4,64,128]{2,1,0:T(8,128)(2,1)} %get-tuple-element.6), channel_id=1, source_target_pairs={{0,1},{1,2},{2,3},{3,4},{4,5},{5,6},{6,7},{7,8},{8,9},{9,10},{10,1... | collective-permute-start | bytes 196616 | tf_op jit(solution)/shard_map/ppermute | solution.py:19
  192.9 28.1 %collective-permute-start.3 = (bf16[4,64,128]{2,1,0:T(8,128)(2,1)S(1)}, bf16[4,64,128]{2,1,0:T(8,128)(2,1)S(1)}, u32[]{:S(2)}, u32[]{:S(2)}) collective-permute-start(bf16[4,64,128]{2,1,0:T(8,128)(2,1)S(1)} %get-tuple-element.7), channel_id=1, source_target_pairs={{1,0},{2,1},{3,2},{4,3},{5,4},{6,5},{7,6},{8,7},{9,8},{10,9},{11,1... | collective-permute-start | bytes 196616 | tf_op jit(solution)/shard_map/ppermute | solution.py:20
  196.9 63.7 %all-to-all-start.2 = ((bf16[256,64,128]{2,1,0:T(8,128)(2,1)}), bf16[256,64,128]{2,1,0:T(8,128)(2,1)}, u32[]{:S(2)}, u32[]{:S(2)}) async-start(bf16[256,64,128]{2,1,0:T(8,128)(2,1)} %broadcast_select_fusion.7), calls=%async_computation.2 | async-start | bytes 8388608 | tf_op jit(solution)/shard_map/all_to_all | solution.py:86
  260.6 107.6 %all-to-all-start.3 = ((f32[256,64,128]{2,1,0:T(8,128)}), f32[256,64,128]{2,1,0:T(8,128)}, u32[]{:S(2)}, u32[]{:S(2)}) async-start(f32[256,64,128]{2,1,0:T(8,128)} %broadcast_select_fusion.4), calls=%async_computation.3 | async-start | bytes 16777216 | tf_op jit(solution)/shard_map/all_to_all | solution.py:95
  270.5 16.0 %slice-start = ((s8[8388608]{0:T(1024)(128)(4,1)}), s8[4194304]{0:T(1024)(128)(4,1)S(1)}, s32[]{:S(2)}) async-start(s8[8388608]{0:T(1024)(128)(4,1)} %bitcast.266), calls=%async_computation.6 | async-start | bytes 8388608
  274.2 12.2 %slice-start.1 = ((s8[8388608]{0:T(1024)(128)(4,1)}), s8[4194304]{0:T(1024)(128)(4,1)S(1)}, s32[]{:S(2)}) async-start(s8[8388608]{0:T(1024)(128)(4,1)} %bitcast.266), calls=%async_computation.7 | async-start | bytes 8388608
  286.4 11.3 %copy-start.31 = (s32[256]{0:T(256)S(1)}, s32[256]{0:T(256)}, u32[]{:S(2)}) copy-start(s32[256]{0:T(256)} %copy-done.30) | copy-start | bytes 3076
  297.8 70.5 %copy-start.25 = (pred[256]{0:T(512)(128)(4,1)S(1)}, pred[256]{0:T(512)(128)(4,1)}, u32[]{:S(2)}) copy-start(pred[256]{0:T(512)(128)(4,1)} %copy-done.24) | copy-start | bytes 772
  336.6 37.6 %copy-start.28 = (s32[256]{0:T(256)S(1)}, s32[256]{0:T(256)}, u32[]{:S(2)}) copy-start(s32[256]{0:T(256)} %copy-done.27) | copy-start | bytes 3076
  374.3 39.0 %copy-start.11 = (f32[64,128]{1,0:T(8,128)S(1)}, f32[64,128]{1,0:T(8,128)}, u32[]{:S(2)}) copy-start(f32[64,128]{1,0:T(8,128)} %copy-done.10) | copy-start | bytes 98308
  582.1 75.7 %collective-permute-start.6 = (bf16[4,64,128]{2,1,0:T(8,128)(2,1)}, bf16[4,64,128]{2,1,0:T(8,128)(2,1)}, u32[]{:S(2)}, u32[]{:S(2)}) collective-permute-start(bf16[4,64,128]{2,1,0:T(8,128)(2,1)} %get-tuple-element.4), channel_id=1, source_target_pairs={{0,1},{1,2},{2,3},{3,4},{4,5},{5,6},{6,7},{7,8},{8,9},{9,10},{10,1... | collective-permute-start | bytes 196616 | tf_op jit(solution)/shard_map/ppermute | solution.py:19
  583.3 28.6 %collective-permute-start.5 = (bf16[4,64,128]{2,1,0:T(8,128)(2,1)S(1)}, bf16[4,64,128]{2,1,0:T(8,128)(2,1)S(1)}, u32[]{:S(2)}, u32[]{:S(2)}) collective-permute-start(bf16[4,64,128]{2,1,0:T(8,128)(2,1)S(1)} %get-tuple-element.5), channel_id=1, source_target_pairs={{1,0},{2,1},{3,2},{4,3},{5,4},{6,5},{7,6},{8,7},{9,8},{10,9},{11,1... | collective-permute-start | bytes 196616 | tf_op jit(solution)/shard_map/ppermute | solution.py:20
  587.5 64.1 %all-to-all-start.4 = ((bf16[256,64,128]{2,1,0:T(8,128)(2,1)}), bf16[256,64,128]{2,1,0:T(8,128)(2,1)}, u32[]{:S(2)}, u32[]{:S(2)}) async-start(bf16[256,64,128]{2,1,0:T(8,128)(2,1)} %broadcast_select_fusion.6), calls=%async_computation.4 | async-start | bytes 8388608 | tf_op jit(solution)/shard_map/all_to_all | solution.py:86
  651.6 107.6 %all-to-all-start.5 = ((f32[256,64,128]{2,1,0:T(8,128)}), f32[256,64,128]{2,1,0:T(8,128)}, u32[]{:S(2)}, u32[]{:S(2)}) async-start(f32[256,64,128]{2,1,0:T(8,128)} %broadcast_select_fusion.1), calls=%async_computation.5 | async-start | bytes 16777216 | tf_op jit(solution)/shard_map/all_to_all | solution.py:95
  661.5 14.7 %slice-start.2 = ((s8[8388608]{0:T(1024)(128)(4,1)}), s8[4194304]{0:T(1024)(128)(4,1)S(1)}, s32[]{:S(2)}) async-start(s8[8388608]{0:T(1024)(128)(4,1)} %bitcast.268), calls=%async_computation.8 | async-start | bytes 8388608
  665.3 10.9 %slice-start.3 = ((s8[8388608]{0:T(1024)(128)(4,1)}), s8[4194304]{0:T(1024)(128)(4,1)S(1)}, s32[]{:S(2)}) async-start(s8[8388608]{0:T(1024)(128)(4,1)} %bitcast.268), calls=%async_computation.9 | async-start | bytes 8388608
  676.2 11.3 %copy-start.32 = (s32[256]{0:T(256)S(1)}, s32[256]{0:T(256)}, u32[]{:S(2)}) copy-start(s32[256]{0:T(256)} %copy-done.30) | copy-start | bytes 3076
  687.5 71.7 %copy-start.26 = (pred[256]{0:T(512)(128)(4,1)S(1)}, pred[256]{0:T(512)(128)(4,1)}, u32[]{:S(2)}) copy-start(pred[256]{0:T(512)(128)(4,1)} %copy-done.24) | copy-start | bytes 772
  713.7 51.5 %copy-start.29 = (s32[256]{0:T(256)S(1)}, s32[256]{0:T(256)}, u32[]{:S(2)}) copy-start(s32[256]{0:T(256)} %copy-done.27) | copy-start | bytes 3076
  765.2 26.1 %copy-start.12 = (f32[64,128]{1,0:T(8,128)S(1)}, f32[64,128]{1,0:T(8,128)}, u32[]{:S(2)}) copy-start(f32[64,128]{1,0:T(8,128)} %copy-done.10) | copy-start | bytes 98308
  (37 other events, 168.4 us)
where the time goes:
time: 962 us; the launch traced here: 953 us
  blocking collectives  326 us (34%)
  other arithmetic  195 us (20%)
  matrix products  189 us (20%)
  waiting for transfers between devices  131 us (14%)
  starting transfers between devices  59.2 us (6%)
  local copies, waits for them, and re-layouts  50.7 us (5%)
    psum x2, blocking collectives, shards(): rayleigh = lax.psum(gram_of(current, image), 'curve') / total_points  134 us
    psum x2, blocking collectives, shards(): cross = lax.psum(gram_of(trial, trial), 'curve') / total_points  126 us
    all_to_all x3, waiting for transfers between devices, apply_w(): lax.all_to_all(mirror, 'curve', split_axis=0, concat_axis=0, tiled=True)  77 us
    scatter-add x3, other arithmetic, apply_w(): result = result.at[send_index].add(jnp.where(send_live, returned, 0.0))  67.2 us
    scatter-add x3, other arithmetic, apply_w(): result = result.at[recv_index].add(jnp.where(recv_live, forward, 0.0))  67.1 us
    psum x1, blocking collectives, shards(): lax.psum(gram_of(start_blocks, start_blocks), 'curve') / total_points  66.3 us
    all_to_all x3, waiting for transfers between devices, apply_w(): lax.all_to_all(outgoing, 'curve', split_axis=0, concat_axis=0, tiled=True)  53.5 us
    dot_general x12, matrix products, near_apply(): jnp.einsum('bcp,bpq->bcq', behind, supers_ext[first:first + rows_dev, ban...  42.3 us
  transfers between devices with their start and end apart: 13, of which 4 were waited for; matrix products, arithmetic and copies ran while one was open for 28% of the time, Pallas kernels for 0%

commit v1 on v0

--- a/solution.py
+++ b/solution.py
@@ -105,7 +105,8 @@
     for step in range(ITERS):
         scaled = (inv_root * current).astype(jnp.bfloat16)
         image = inv_root * apply_w(scaled)
-        rayleigh = lax.psum(gram_of(current, image), "curve") / total_points
+        see_row = lambda x_local: lax.all_gather(x_local, "curve").sum(axis=0)
+        rayleigh = see_row(gram_of(current, image)) / total_points
         resid = image - left_apply(rayleigh.T, current)
         trial = current + step_size * resid + momentum * change
         cross = lax.psum(gram_of(trial, trial), "curve") / total_points

time: 962 us -> 987 us (1.026)
  waiting for transfers between devices: 131 us -> 268 us
  blocking collectives: 326 us -> 192 us
  between operations: 1.56 us -> 15.3 us
    all_gather x0 -> x2, waiting for transfers between devices: none -> 141 us  [shards(): see_row = lambda x_local: lax.all_gather(x_local, 'curve').sum(axis=0)]
    psum x2 -> x0, blocking collectives: 134 us -> none  [shards(): rayleigh = lax.psum(gram_of(current, image), 'curve') / total_points]
  transfers between devices with their start and end apart: 13 -> 15, of which waited for: 4 -> 6; matrix products, arithmetic and copies ran while one was open for 28% -> 27% of each run, Pallas kernels for 0% -> 0%
where the time goes in v1:
time: 987 us; the launch traced here: 978 us
  waiting for transfers between devices  268 us (27%)
  other arithmetic  202 us (20%)
  blocking collectives  192 us (19%)
  matrix products  191 us (19%)
  starting transfers between devices  58.8 us (6%)
  local copies, waits for them, and re-layouts  51 us (5%)
  between operations  15.3 us (2%)
    all_gather x2, waiting for transfers between devices, shards(): see_row = lambda x_local: lax.all_gather(x_local, 'curve').sum(axis=0)  141 us
    psum x2, blocking collectives, shards(): cross = lax.psum(gram_of(trial, trial), 'curve') / total_points  125 us
    all_to_all x3, waiting for transfers between devices, apply_w(): lax.all_to_all(mirror, 'curve', split_axis=0, concat_axis=0, tiled=True)  73.7 us
    scatter-add x3, other arithmetic, apply_w(): result = result.at[recv_index].add(jnp.where(recv_live, forward, 0.0))  68.8 us
    scatter-add x3, other arithmetic, apply_w(): result = result.at[send_index].add(jnp.where(send_live, returned, 0.0))  67.2 us
    psum x1, blocking collectives, shards(): lax.psum(gram_of(start_blocks, start_blocks), 'curve') / total_points  66.3 us
    all_to_all x3, waiting for transfers between devices, apply_w(): lax.all_to_all(outgoing, 'curve', split_axis=0, concat_axis=0, tiled=True)  53.2 us
    dot_general x12, matrix products, near_apply(): jnp.einsum('bcp,bpq->bcq', behind, supers_ext[first:first + rows_dev, ban...  42.3 us
  transfers between devices with their start and end apart: 15, of which 6 were waited for; matrix products, arithmetic and copies ran while one was open for 27% of the time, Pallas kernels for 0%

profile of v1, /device:TPU:1, one launch (start us, length us, event | category | flops | bytes accessed | tf_op | source)
XLA Modules:
  0.0 977.6 jit_solution(4233618599151227738)
XLA Ops:
  14.1 10.2 %all-to-all-start = ((bf16[128,2,128]{2,1,0:T(2,128)(2,1)}), bf16[128,2,128]{2,1,0:T(2,128)(2,1)S(1)}, u32[]{:S(2)}, u32[]{:S(2)}) async-start(bf16[128,2,128]{2,1,0:T(2,128)(2,1)} %bitcast.267), calls=%async_computation | async-start | bytes 131072 | tf_op jit(solution)/shard_map/all_to_all | solution.py:86
  24.3 10.4 %copy.58 = bf16[64,4,128,128]{3,2,0,1:T(8,128)(2,1)} copy(bf16[64,4,128,128]{3,2,1,0:T(8,128)(2,1)} %param.10) | data formatting | bytes 16777216 | tf_op args[1]
  42.5 66.3 %psum.21 = f32[64,64]{0,1:T(8,128)S(1)} all-reduce(f32[64,64]{0,1:T(8,128)S(1)} %fusion.51), channel_id=1, replica_groups=mesh['curve'=128] {'curve'}, use_global_device_ids=true, to_apply=%region_0.1 | all-reduce | flops 4096 | bytes 32768 | tf_op jit(solution)/shard_map/psum | solution.py:102
  108.9 5.8 cholesky.59
  144.0 6.0 all-to-all-start.1
  150.8 7.8 fusion.66
  159.6 10.5 %constant_dynamic-update-slice_fusion = bf16[68,4,128,128]{3,2,0,1:T(8,128)(2,1)} fusion(bf16[68,4,128,128]{3,2,0,1:T(8,128)(2,1)} %constant_dynamic-update-slice_fusion.1, bf16[64,4,128,128]{3,2,1,0:T(8,128)(2,1)} %param.10), kind=kLoop, calls=%fused_computation.180 | loop fusion | bytes 16777216 | tf_op jit(solution)/shard_map/concatenate | solution.py:50
  203.5 11.0 %all-to-all-start.2 = ((bf16[256,64,128]{2,1,0:T(8,128)(2,1)}), bf16[256,64,128]{2,1,0:T(8,128)(2,1)}, u32[]{:S(2)}, u32[]{:S(2)}) async-start(bf16[256,64,128]{2,1,0:T(8,128)(2,1)} %broadcast_select_fusion.7), calls=%async_computation.2 | async-start | bytes 8388608 | tf_op jit(solution)/shard_map/all_to_all | solution.py:86
  214.5 10.3 %broadcast_select_fusion.4 = f32[256,64,128]{2,1,0:T(8,128)} fusion(pred[256]{0:T(512)(128)(4,1)S(1)} %broadcast_compare_fusion.1, bf16[256,64,128]{2,1,0:T(8,128)(2,1)} %gather_fusion.3, bf16[256,128,128]{2,1,0:T(8,128)(2,1)} %param.11), kind=kOutput, calls=%fused_computation.16 | convolution fusion | flops 538968064 | bytes 20971776 | tf_op jit(solution)/shard_map/fcp,fpq->fcq/dot_general | solution.py:91
  240.6 26.7 %all-to-all-done.2 = bf16[256,64,128]{2,1,0:T(8,128)(2,1)} async-done(((bf16[256,64,128]{2,1,0:T(8,128)(2,1)}), bf16[256,64,128]{2,1,0:T(8,128)(2,1)}, u32[]{:S(2)}, u32[]{:S(2)}) %all-to-all-start.2) | async-done | bytes 4194336 | tf_op jit(solution)/shard_map/all_to_all | solution.py:86
  267.3 5.7 all-to-all-start.3
  286.7 6.1 add_add_fusion.1
  292.9 11.3 %broadcast_select_fusion.5 = f32[256,64,128]{2,1,0:T(8,128)} fusion(pred[256]{0:T(512)(128)(4,1)S(1)} %copy-done.18, bf16[256,64,128]{2,1,0:T(8,128)(2,1)} %all-to-all-done.2, bf16[256,128,128]{2,1,0:T(8,128)(2,1)S(1)} %bitcast.269), kind=kOutput, calls=%fused_computation.17 | convolution fusion | flops 538968064 | bytes 20971776 | tf_op jit(solution)/shard_map/fcp,fqp->fcq/dot_general | solution.py:87
  304.2 40.3 %scatter_fusion = f32[64,64,128]{2,1,0:T(8,128)} fusion(f32[64,64,128]{2,1,0:T(8,128)} %add_add_fusion.1, s32[256]{0:T(256)S(1)} %copy-done.31, f32[256,64,128]{2,1,0:T(8,128)} %broadcast_select_fusion.5), kind=kCustom, calls=%fused_computation.8 | custom fusion | flops 2097152 | bytes 25166848 | tf_op jit(solution)/shard_map/scatter-add | solution.py:90
  344.4 29.3 %all-to-all-done.3 = f32[256,64,128]{2,1,0:T(8,128)} async-done(((f32[256,64,128]{2,1,0:T(8,128)}), f32[256,64,128]{2,1,0:T(8,128)}, u32[]{:S(2)}, u32[]{:S(2)}) %all-to-all-start.3) | async-done | bytes 8388640 | tf_op jit(solution)/shard_map/all_to_all | solution.py:95
  373.8 6.1 broadcast_select_fusion.3
  379.9 39.0 %scatter_fusion.1 = f32[64,64,128]{2,1,0:T(8,128)} fusion(f32[64,64,128]{2,1,0:T(8,128)} %scatter_fusion, s32[256]{0:T(256)S(1)} %copy-done.28, f32[256,64,128]{2,1,0:T(8,128)} %broadcast_select_fusion.3), kind=kCustom, calls=%fused_computation.9 | custom fusion | flops 2097152 | bytes 25166848 | tf_op jit(solution)/shard_map/scatter-add | solution.py:96
  423.6 71.6 %all-gather.5.cloned.1.call-done = f32[8192,64]{1,0:T(8,128)} async-done(((f32[64,64]{1,0:T(8,128)}), f32[8192,64]{1,0:T(8,128)}) %all-gather.5.cloned.1.call-update) | async-done | bytes 2097168 | tf_op jit(solution)/shard_map/all_gather | solution.py:108
  506.0 62.7 %psum.22 = f32[64,64]{0,1:T(8,128)S(1)} all-reduce(f32[64,64]{0,1:T(8,128)S(1)} %convolution_bitcast_fusion.3), channel_id=1, replica_groups=mesh['curve'=128] {'curve'}, use_global_device_ids=true, to_apply=%region_8.11 | all-reduce | flops 4096 | bytes 32768 | tf_op jit(solution)/shard_map/psum | solution.py:112
  568.8 5.8 cholesky.70
  601.2 11.1 %all-to-all-start.4 = ((bf16[256,64,128]{2,1,0:T(8,128)(2,1)}), bf16[256,64,128]{2,1,0:T(8,128)(2,1)}, u32[]{:S(2)}, u32[]{:S(2)}) async-start(bf16[256,64,128]{2,1,0:T(8,128)(2,1)} %broadcast_select_fusion.6), calls=%async_computation.4 | async-start | bytes 8388608 | tf_op jit(solution)/shard_map/all_to_all | solution.py:86
  612.3 10.3 %broadcast_select_fusion.1 = f32[256,64,128]{2,1,0:T(8,128)} fusion(pred[256]{0:T(512)(128)(4,1)S(1)} %copy-done.18, bf16[256,64,128]{2,1,0:T(8,128)(2,1)} %gather_fusion.5, bf16[256,128,128]{2,1,0:T(8,128)(2,1)} %param.11), kind=kOutput, calls=%fused_computation.13 | convolution fusion | flops 538968064 | bytes 20971776 | tf_op jit(solution)/shard_map/fcp,fpq->fcq/dot_general | solution.py:91
  638.3 26.5 %all-to-all-done.4 = bf16[256,64,128]{2,1,0:T(8,128)(2,1)} async-done(((bf16[256,64,128]{2,1,0:T(8,128)(2,1)}), bf16[256,64,128]{2,1,0:T(8,128)(2,1)}, u32[]{:S(2)}, u32[]{:S(2)}) %all-to-all-start.4) | async-done | bytes 4194336 | tf_op jit(solution)/shard_map/all_to_all | solution.py:86
  664.9 5.7 all-to-all-start.5
  689.2 11.3 %broadcast_select_fusion.2 = f32[256,64,128]{2,1,0:T(8,128)} fusion(pred[256]{0:T(512)(128)(4,1)S(1)} %copy-done.19, bf16[256,64,128]{2,1,0:T(8,128)(2,1)} %all-to-all-done.4, bf16[256,128,128]{2,1,0:T(8,128)(2,1)S(1)} %bitcast.271), kind=kOutput, calls=%fused_computation.14 | convolution fusion | flops 538968064 | bytes 20971776 | tf_op jit(solution)/shard_map/fcp,fqp->fcq/dot_general | solution.py:87
  700.6 26.5 %scatter_fusion.2 = f32[64,64,128]{2,1,0:T(8,128)S(1)} fusion(f32[64,64,128]{2,1,0:T(8,128)S(1)} %add_add_fusion, s32[256]{0:T(256)S(1)} %copy-done.32, f32[256,64,128]{2,1,0:T(8,128)} %broadcast_select_fusion.2), kind=kCustom, calls=%fused_computation.10 | custom fusion | flops 2097152 | bytes 25166848 | tf_op jit(solution)/shard_map/scatter-add | solution.py:90
  727.1 44.3 %all-to-all-done.5 = f32[256,64,128]{2,1,0:T(8,128)} async-done(((f32[256,64,128]{2,1,0:T(8,128)}), f32[256,64,128]{2,1,0:T(8,128)}, u32[]{:S(2)}, u32[]{:S(2)}) %all-to-all-start.5) | async-done | bytes 8388640 | tf_op jit(solution)/shard_map/all_to_all | solution.py:95
  771.4 6.0 broadcast_select_fusion
  777.4 26.1 %scatter_fusion.3 = f32[64,64,128]{2,1,0:T(8,128)S(1)} fusion(f32[64,64,128]{2,1,0:T(8,128)S(1)} %scatter_fusion.2, s32[256]{0:T(256)S(1)} %copy-done.29, f32[256,64,128]{2,1,0:T(8,128)} %broadcast_select_fusion), kind=kCustom, calls=%fused_computation.11 | custom fusion | flops 2097152 | bytes 25166848 | tf_op jit(solution)/shard_map/scatter-add | solution.py:96
  807.7 69.4 %all-gather.7.cloned.1.call-done = f32[8192,64]{1,0:T(8,128)} async-done(((f32[64,64]{1,0:T(8,128)}), f32[8192,64]{1,0:T(8,128)}) %all-gather.7.cloned.1.call-update) | async-done | bytes 2097168 | tf_op jit(solution)/shard_map/all_gather | solution.py:108
  888.3 62.8 %psum.23 = f32[64,64]{0,1:T(8,128)S(1)} all-reduce(f32[64,64]{0,1:T(8,128)S(1)} %convolution_bitcast_fusion.1), channel_id=1, replica_groups=mesh['curve'=128] {'curve'}, use_global_device_ids=true, to_apply=%region_12.15 | all-reduce | flops 4096 | bytes 32768 | tf_op jit(solution)/shard_map/psum | solution.py:112
  951.2 5.8 cholesky.81
  (236 shorter events, 213.3 us)
Async XLA Ops:
  7.2 30.5 %copy-start = (bf16[64,128,128]{2,1,0:T(8,128)(2,1)S(1)}, bf16[64,128,128]{2,1,0:T(8,128)(2,1)}, u32[]{:S(2)}) copy-start(bf16[64,128,128]{2,1,0:T(8,128)(2,1)} %param.9) | copy-start | bytes 6291460
  7.2 135.5 %collective-permute-start.1 = (bf16[4,1,128]{2,0,1:T(4,128)(2,1)S(1)}, bf16[4,1,128]{2,0,1:T(4,128)(2,1)S(1)}, u32[]{:S(2)}, u32[]{:S(2)}) collective-permute-start(bf16[4,1,128]{2,0,1:T(4,128)(2,1)S(1)} %broadcast.92), channel_id=1, source_target_pairs={{0,1},{1,2},{2,3},{3,4},{4,5},{5,6},{6,7},{7,8},{8,9},{9,10},{10,1... | collective-permute-start | bytes 3080 | tf_op jit(solution)/shard_map/ppermute | solution.py:19
  10.3 118.8 %collective-permute-start = (bf16[4,1,128]{2,0,1:T(4,128)(2,1)S(1)}, bf16[4,1,128]{2,0,1:T(4,128)(2,1)S(1)}, u32[]{:S(2)}, u32[]{:S(2)}) collective-permute-start(bf16[4,1,128]{2,0,1:T(4,128)(2,1)S(1)} %broadcast.92), channel_id=1, source_target_pairs={{1,0},{2,1},{3,2},{4,3},{5,4},{6,5},{7,6},{8,7},{9,8},{10,9},{11,1... | collective-permute-start | bytes 3080 | tf_op jit(solution)/shard_map/ppermute | solution.py:20
  11.0 188.6 %copy-start.24 = (pred[256]{0:T(512)(128)(4,1)}, pred[256]{0:T(512)(128)(4,1)S(1)}, u32[]{:S(2)}) copy-start(pred[256]{0:T(512)(128)(4,1)S(1)} %broadcast_compare_fusion) | copy-start | bytes 772
  11.7 169.7 %copy-start.27 = (s32[256]{0:T(256)}, s32[256]{0:T(256)S(1)}, u32[]{:S(2)}) copy-start(s32[256]{0:T(256)S(1)} %broadcast_maximum_fusion) | copy-start | bytes 3076
  12.3 166.9 %copy-start.30 = (s32[256]{0:T(256)}, s32[256]{0:T(256)S(1)}, u32[]{:S(2)}) copy-start(s32[256]{0:T(256)S(1)} %broadcast_maximum_fusion.1) | copy-start | bytes 3076
  12.4 108.6 %copy-start.38 = (s32[1024]{0:T(1024)}, s32[1024]{0:T(1024)S(1)}, u32[]{:S(2)}) copy-start(s32[1024]{0:T(1024)S(1)} %get-tuple-element.20) | copy-start | bytes 12292
  14.1 129.2 %all-to-all-start = ((bf16[128,2,128]{2,1,0:T(2,128)(2,1)}), bf16[128,2,128]{2,1,0:T(2,128)(2,1)S(1)}, u32[]{:S(2)}, u32[]{:S(2)}) async-start(bf16[128,2,128]{2,1,0:T(2,128)(2,1)} %bitcast.267), calls=%async_computation | async-start | bytes 131072 | tf_op jit(solution)/shard_map/all_to_all | solution.py:86
  24.3 13.3 %copy-start.39 = (s32[256]{0:T(256)S(1)}, s32[256]{0:T(256)}, u32[]{:S(2)}) copy-start(s32[256]{0:T(256)} %param.12) | copy-start | bytes 3076
  35.8 122.8 %collective-permute-start.2 = (bf16[4,4,128,128]{3,2,0,1:T(8,128)(2,1)S(1)}, bf16[4,4,128,128]{3,2,0,1:T(8,128)(2,1)S(1)}, u32[]{:S(2)}, u32[]{:S(2)}) collective-permute-start(bf16[4,4,128,128]{3,2,0,1:T(8,128)(2,1)S(1)} %slice.207), channel_id=1, source_target_pairs={{127,0},{0,1},{1,2},{2,3},{3,4},{4,5},{5,6},{6,7},{7,8},{8,9},{9,1... | collective-permute-start | bytes 1572872 | tf_op jit(solution)/shard_map/ppermute | solution.py:28
  37.7 176.8 %copy-start.17 = (pred[256]{0:T(512)(128)(4,1)}, pred[256]{0:T(512)(128)(4,1)S(1)}, u32[]{:S(2)}) copy-start(pred[256]{0:T(512)(128)(4,1)S(1)} %broadcast_compare_fusion.1) | copy-start | bytes 772
  144.0 37.4 %all-to-all-start.1 = ((f32[256,1,128]{2,1,0:T(1,128)}), f32[256,1,128]{2,1,0:T(1,128)S(1)}, u32[]{:S(2)}, u32[]{:S(2)}) async-start(f32[256,1,128]{2,1,0:T(1,128)} %bitcast.58), calls=%async_computation.1 | async-start | bytes 262144 | tf_op jit(solution)/shard_map/all_to_all | solution.py:95
  197.5 75.7 %collective-permute-start.4 = (bf16[4,64,128]{2,1,0:T(8,128)(2,1)}, bf16[4,64,128]{2,1,0:T(8,128)(2,1)}, u32[]{:S(2)}, u32[]{:S(2)}) collective-permute-start(bf16[4,64,128]{2,1,0:T(8,128)(2,1)} %get-tuple-element.6), channel_id=1, source_target_pairs={{0,1},{1,2},{2,3},{3,4},{4,5},{5,6},{6,7},{7,8},{8,9},{9,10},{10,1... | collective-permute-start | bytes 196616 | tf_op jit(solution)/shard_map/ppermute | solution.py:19
  199.5 28.2 %collective-permute-start.3 = (bf16[4,64,128]{2,1,0:T(8,128)(2,1)S(1)}, bf16[4,64,128]{2,1,0:T(8,128)(2,1)S(1)}, u32[]{:S(2)}, u32[]{:S(2)}) collective-permute-start(bf16[4,64,128]{2,1,0:T(8,128)(2,1)S(1)} %get-tuple-element.7), channel_id=1, source_target_pairs={{1,0},{2,1},{3,2},{4,3},{5,4},{6,5},{7,6},{8,7},{9,8},{10,9},{11,1... | collective-permute-start | bytes 196616 | tf_op jit(solution)/shard_map/ppermute | solution.py:20
  203.5 63.7 %all-to-all-start.2 = ((bf16[256,64,128]{2,1,0:T(8,128)(2,1)}), bf16[256,64,128]{2,1,0:T(8,128)(2,1)}, u32[]{:S(2)}, u32[]{:S(2)}) async-start(bf16[256,64,128]{2,1,0:T(8,128)(2,1)} %broadcast_select_fusion.7), calls=%async_computation.2 | async-start | bytes 8388608 | tf_op jit(solution)/shard_map/all_to_all | solution.py:86
  267.3 106.5 %all-to-all-start.3 = ((f32[256,64,128]{2,1,0:T(8,128)}), f32[256,64,128]{2,1,0:T(8,128)}, u32[]{:S(2)}, u32[]{:S(2)}) async-start(f32[256,64,128]{2,1,0:T(8,128)} %broadcast_select_fusion.4), calls=%async_computation.3 | async-start | bytes 16777216 | tf_op jit(solution)/shard_map/all_to_all | solution.py:95
  272.9 222.2 %all-gather.5.cloned.1.call-start = ((), (), s32[]{:S(2)}) async-start(), calls=%async_computation.6 | async-start | bytes 4227072 | tf_op jit(solution)/shard_map/all_gather | solution.py:108
  276.9 16.0 %slice-start = ((s8[8388608]{0:T(1024)(128)(4,1)}), s8[4194304]{0:T(1024)(128)(4,1)S(1)}, s32[]{:S(2)}) async-start(s8[8388608]{0:T(1024)(128)(4,1)} %bitcast.268), calls=%async_computation.8 | async-start | bytes 8388608
  280.6 12.2 %slice-start.1 = ((s8[8388608]{0:T(1024)(128)(4,1)}), s8[4194304]{0:T(1024)(128)(4,1)S(1)}, s32[]{:S(2)}) async-start(s8[8388608]{0:T(1024)(128)(4,1)} %bitcast.268), calls=%async_computation.9 | async-start | bytes 8388608
  292.8 11.3 %copy-start.31 = (s32[256]{0:T(256)S(1)}, s32[256]{0:T(256)}, u32[]{:S(2)}) copy-start(s32[256]{0:T(256)} %copy-done.30) | copy-start | bytes 3076
  304.2 69.6 %copy-start.25 = (pred[256]{0:T(512)(128)(4,1)S(1)}, pred[256]{0:T(512)(128)(4,1)}, u32[]{:S(2)}) copy-start(pred[256]{0:T(512)(128)(4,1)} %copy-done.24) | copy-start | bytes 772
  344.4 35.4 %copy-start.28 = (s32[256]{0:T(256)S(1)}, s32[256]{0:T(256)}, u32[]{:S(2)}) copy-start(s32[256]{0:T(256)} %copy-done.27) | copy-start | bytes 3076
  379.9 39.0 %copy-start.11 = (f32[64,128]{1,0:T(8,128)S(1)}, f32[64,128]{1,0:T(8,128)}, u32[]{:S(2)}) copy-start(f32[64,128]{1,0:T(8,128)} %copy-done.10) | copy-start | bytes 98308
  595.4 75.5 %collective-permute-start.6 = (bf16[4,64,128]{2,1,0:T(8,128)(2,1)}, bf16[4,64,128]{2,1,0:T(8,128)(2,1)}, u32[]{:S(2)}, u32[]{:S(2)}) collective-permute-start(bf16[4,64,128]{2,1,0:T(8,128)(2,1)} %get-tuple-element.4), channel_id=1, source_target_pairs={{0,1},{1,2},{2,3},{3,4},{4,5},{5,6},{6,7},{7,8},{8,9},{9,10},{10,1... | collective-permute-start | bytes 196616 | tf_op jit(solution)/shard_map/ppermute | solution.py:19
  597.1 28.4 %collective-permute-start.5 = (bf16[4,64,128]{2,1,0:T(8,128)(2,1)S(1)}, bf16[4,64,128]{2,1,0:T(8,128)(2,1)S(1)}, u32[]{:S(2)}, u32[]{:S(2)}) collective-permute-start(bf16[4,64,128]{2,1,0:T(8,128)(2,1)S(1)} %get-tuple-element.5), channel_id=1, source_target_pairs={{1,0},{2,1},{3,2},{4,3},{5,4},{6,5},{7,6},{8,7},{9,8},{10,9},{11,1... | collective-permute-start | bytes 196616 | tf_op jit(solution)/shard_map/ppermute | solution.py:20
  601.2 63.7 %all-to-all-start.4 = ((bf16[256,64,128]{2,1,0:T(8,128)(2,1)}), bf16[256,64,128]{2,1,0:T(8,128)(2,1)}, u32[]{:S(2)}, u32[]{:S(2)}) async-start(bf16[256,64,128]{2,1,0:T(8,128)(2,1)} %broadcast_select_fusion.6), calls=%async_computation.4 | async-start | bytes 8388608 | tf_op jit(solution)/shard_map/all_to_all | solution.py:86
  664.9 106.5 %all-to-all-start.5 = ((f32[256,64,128]{2,1,0:T(8,128)}), f32[256,64,128]{2,1,0:T(8,128)}, u32[]{:S(2)}, u32[]{:S(2)}) async-start(f32[256,64,128]{2,1,0:T(8,128)} %broadcast_select_fusion.1), calls=%async_computation.5 | async-start | bytes 16777216 | tf_op jit(solution)/shard_map/all_to_all | solution.py:95
  670.6 206.6 %all-gather.7.cloned.1.call-start = ((), (), s32[]{:S(2)}) async-start(), calls=%async_computation.7 | async-start | bytes 4227072 | tf_op jit(solution)/shard_map/all_gather | solution.py:108
  674.5 14.7 %slice-start.2 = ((s8[8388608]{0:T(1024)(128)(4,1)}), s8[4194304]{0:T(1024)(128)(4,1)S(1)}, s32[]{:S(2)}) async-start(s8[8388608]{0:T(1024)(128)(4,1)} %bitcast.270), calls=%async_computation.10 | async-start | bytes 8388608
  700.5 70.9 %copy-start.26 = (pred[256]{0:T(512)(128)(4,1)S(1)}, pred[256]{0:T(512)(128)(4,1)}, u32[]{:S(2)}) copy-start(pred[256]{0:T(512)(128)(4,1)} %copy-done.24) | copy-start | bytes 772
  727.1 50.4 %copy-start.29 = (s32[256]{0:T(256)S(1)}, s32[256]{0:T(256)}, u32[]{:S(2)}) copy-start(s32[256]{0:T(256)} %copy-done.27) | copy-start | bytes 3076
  777.4 26.1 %copy-start.12 = (f32[64,128]{1,0:T(8,128)S(1)}, f32[64,128]{1,0:T(8,128)}, u32[]{:S(2)}) copy-start(f32[64,128]{1,0:T(8,128)} %copy-done.10) | copy-start | bytes 98308
  (39 other events, 190.6 us)
Sparse Core Ops, SparseCore 0:
  423.7 71.4 all-gather.4
  807.8 69.2 all-gather.6
